TPU v7x, 32 devices: a whole 2x2x4 slice. The times are simulated.
32 devices in a mesh: dp: 4 (over y, x), expert: 8 (over z, core).
Axes of the slice: x: 2, y: 2, z: 4, core: 2. Of those that a mesh axis runs over, the one named last changes fastest.
Arguments:
- tokens: bfloat16 [32768, 768], P(('dp', 'expert')), may hold values from -6 to 6
- cotangent: bfloat16 [32768, 768], P(('dp', 'expert')), may hold values from -6 to 6
- seg_start: int32 [32768], P(('dp', 'expert')), may hold values from 0 to 1023, as said below
- dispatch_slot: int32 [32768], P(('dp', 'expert')), may hold values from 0 to 2048, as said below
- ln1_gain: float32 [768], replicated, may hold values from 0.25 to 1.75
- ln1_shift: float32 [768], replicated, may hold values from -3 to 3
- w_qkv: bfloat16 [768, 2304], replicated, may hold values from -0.21875 to 0.21875
- w_attn_out: bfloat16 [768, 768], replicated, may hold values from -0.875 to 0.875
- ln2_gain: float32 [768], replicated, may hold values from 0.25 to 1.75
- ln2_shift: float32 [768], replicated, may hold values from -3 to 3
- w_in: bfloat16 [2, 768, 3072], replicated, may hold values from -0.21875 to 0.21875
- w_out: bfloat16 [2, 3072, 768], replicated, may hold values from -0.109375 to 0.109375
Outputs:
- result_out: bfloat16 [32768, 768], P(('dp', 'expert'))
- grad_tokens: float32 [32768, 768], P(('dp', 'expert'))
- grad_ln1_gain: float32 [768], replicated
- grad_ln1_shift: float32 [768], replicated
- grad_w_qkv: float32 [768, 2304], replicated
- grad_w_attn_out: float32 [768, 768], replicated
- grad_ln2_gain: float32 [768], replicated
- grad_ln2_shift: float32 [768], replicated
- grad_w_in: float32 [2, 768, 3072], P(None, None, 'expert')
- grad_w_out: float32 [2, 3072, 768], P(None, 'expert')
- expert_counts: int32 [2], replicated
Inputs may be any that keep to these rules, and one draw needn't show every extreme that they name: A row is an image row or a caption row. An image row's first 985 slots hold 5 images of 197 patches each, its other slots are padding, each padding token a segment of its own; a caption row is filled with captions. A token attends only to tokens of its own row with the same seg_start. `dispatch_slot`: slot s sends the token to the device at expert index s // 256 of its dp index, at place s % 256. Image tokens go to expert indices below 4, caption tokens to the others; no two tokens of one device share a slot; padding tokens, and only they, have s = 2048.
All inputs are finite; a program needn't handle non-finite values.
Results may differ from a plain program's by a relative error of at most 0.012.
Values may be sent and summed in bfloat16 or wider, within the bound.
No kernel may reach another device: no remote copies, remote signals or barrier semaphores. Data moves between devices by JAX's collectives and lax.ppermute only.
A program may use at most 320 MiB of HBM per device.

v0:
```python
import math
import jax
import jax.numpy as jnp
from jax import lax
from jax.sharding import PartitionSpec as P

HEADS = 12
DH = 64
FF = 3072
LEN = 1024
EPS = 1e-05
NEG = -1e30


def layer_norm(values, gain_vec, shift_vec):
    row_mean = jnp.mean(values, axis=-1, keepdims=True)
    centred = values - row_mean
    variance = jnp.mean(centred * centred, axis=-1, keepdims=True)
    return centred * lax.rsqrt(variance + EPS) * gain_vec + shift_vec


def gelu_exact(values):
    return jax.nn.gelu(values, approximate=False)


def contract_rows(first_op, second_op):
    return lax.dot_general(
        first_op, second_op, (((0,), (0,)), ((), ())), preferred_element_type=jnp.float32
    )


def contract_cols(first_op, second_op):
    return lax.dot_general(
        first_op, second_op, (((1,), (1,)), ((), ())), preferred_element_type=jnp.float32
    )


def row_pieces(qkv_b, seg_start, block_start, qblock):
    row_start = block_start // LEN * LEN
    query_rows = lax.dynamic_slice_in_dim(qkv_b, block_start, qblock, 0).reshape(
        qblock, 3, HEADS, DH
    )
    row_all = qkv_b.reshape(LEN, 3, HEADS, DH)
    seg_query = lax.dynamic_slice_in_dim(seg_start, block_start, qblock, 0)
    allowed = seg_query[:, None] == seg_start[None, :]
    score_scale = 1.0 / math.sqrt(DH)
    scores = (
        jnp.einsum(
            "qhd,khd->hqk", query_rows[:, 0], row_all[:, 1], preferred_element_type=jnp.float32
        )
        * score_scale
    )
    scores = jnp.where(allowed[None], scores, NEG)
    return (query_rows[:, 0], row_all[:, 1], row_all[:, 2], row_start, scores)


def shards(
    tokens,
    cotangent,
    seg_start,
    dispatch_slot,
    ln1_gain,
    ln1_shift,
    w_qkv,
    w_attn_out,
    ln2_gain,
    ln2_shift,
    w_in,
    w_out,
):
    tok_count = tokens.shape[0]
    feat_width = tokens.shape[1]
    n_expert = lax.axis_size("expert")
    group_size = n_expert // 2
    capacity = 2 * tok_count // n_expert
    n_slots = n_expert * capacity
    qblock = min(512, LEN)
    n_blocks = tok_count // qblock
    score_scale = 1.0 / math.sqrt(DH)
    own_expert = lax.axis_index("expert") // group_size
    inputs = tokens.astype(jnp.float32)
    normed_one, ln1_back = jax.vjp(layer_norm, inputs, ln1_gain, ln1_shift)
    normed_one_b = normed_one.astype(jnp.bfloat16)
    qkv_b = jnp.dot(normed_one_b, w_qkv, preferred_element_type=jnp.float32).astype(jnp.bfloat16)

    def forward_block(block_index):
        block_start = block_index * qblock
        queries, keys_row, values_row, row_start, scores = row_pieces(
            qkv_b, seg_start, block_start, qblock
        )
        top_score = jnp.max(scores, axis=-1, keepdims=True)
        shifted = jnp.exp(scores - top_score)
        totals = jnp.sum(shifted, axis=-1, keepdims=True)
        probs_b = (shifted / totals).astype(jnp.bfloat16)
        mixed_rows = jnp.einsum(
            "hqk,khd->qhd", probs_b, values_row, preferred_element_type=jnp.float32
        )
        return (
            mixed_rows.reshape(qblock, feat_width).astype(jnp.bfloat16),
            (top_score + jnp.log(totals))[..., 0],
        )

    mixed_blocks, lse_all = lax.map(forward_block, jnp.arange(n_blocks, dtype=jnp.int32))
    mixed_b = mixed_blocks.reshape(tok_count, feat_width)
    residual = inputs + jnp.dot(mixed_b, w_attn_out, preferred_element_type=jnp.float32)
    normed_two, ln2_back = jax.vjp(layer_norm, residual, ln2_gain, ln2_shift)
    normed_two_b = normed_two.astype(jnp.bfloat16)
    positions = jnp.arange(tok_count, dtype=jnp.int32)
    source_of = (
        jnp.full((n_slots,), tok_count, jnp.int32).at[dispatch_slot].set(positions, mode="drop")
    )
    zero_row = jnp.zeros((1, feat_width), jnp.bfloat16)
    send_rows = jnp.take(
        jnp.concatenate([normed_two_b, zero_row], axis=0), source_of, axis=0
    ).reshape(n_expert, capacity, feat_width)
    expert_in = lax.dynamic_index_in_dim(w_in, own_expert, 0, keepdims=False)
    expert_out = lax.dynamic_index_in_dim(w_out, own_expert, 0, keepdims=False)
    received = lax.all_to_all(send_rows, "expert", split_axis=0, concat_axis=0, tiled=True)
    flat_rows = received.reshape(-1, feat_width)
    hidden_pre = jnp.dot(flat_rows, expert_in, preferred_element_type=jnp.float32)
    hidden_b = gelu_exact(hidden_pre).astype(jnp.bfloat16)
    result = jnp.dot(hidden_b, expert_out, preferred_element_type=jnp.float32).astype(jnp.bfloat16)
    shape_lead = received.shape[:2]
    expert_rows_b, hidden_pre, received = (
        result.reshape(received.shape),
        hidden_pre.reshape(shape_lead + (FF,)),
        received,
    )
    returned = lax.all_to_all(expert_rows_b, "expert", split_axis=0, concat_axis=0, tiled=True)
    ffn_tok = jnp.take(
        jnp.concatenate([returned.reshape(n_slots, feat_width), zero_row], axis=0),
        dispatch_slot,
        axis=0,
    )
    result_out = (residual + ffn_tok.astype(jnp.float32)).astype(jnp.bfloat16)
    grad_out = cotangent.astype(jnp.float32)
    grad_send = jnp.take(jnp.concatenate([cotangent, zero_row], axis=0), source_of, axis=0).reshape(
        n_expert, capacity, feat_width
    )
    grad_expert = lax.all_to_all(grad_send, "expert", split_axis=0, concat_axis=0, tiled=True)
    grad_flat = grad_expert.reshape(n_slots, feat_width)
    rows_flat = received.reshape(n_slots, feat_width)
    pre_flat = hidden_pre.reshape(n_slots, FF)
    hidden_value, gelu_back = jax.vjp(gelu_exact, pre_flat)
    d_hidden = contract_cols(grad_flat, expert_out)
    d_pre_b = gelu_back(d_hidden)[0].astype(jnp.bfloat16)
    d_rows = contract_cols(d_pre_b, expert_in).astype(jnp.bfloat16)
    grad_back = lax.all_to_all(
        d_rows.reshape(n_expert, capacity, feat_width),
        "expert",
        split_axis=0,
        concat_axis=0,
        tiled=True,
    )
    d_normed_two = jnp.take(
        jnp.concatenate([grad_back.reshape(n_slots, feat_width), zero_row], axis=0),
        dispatch_slot,
        axis=0,
    ).astype(jnp.float32)
    part_in_t = contract_rows(d_pre_b, rows_flat)
    part_out = contract_rows(hidden_value.astype(jnp.bfloat16), grad_flat)
    which = (jnp.arange(2, dtype=jnp.int32) == own_expert)[:, None, None]
    padded_in = jnp.where(which, part_in_t[None], 0.0)
    padded_out = jnp.where(which, part_out[None], 0.0)
    group_in_t, group_out = (
        lax.psum_scatter(padded_in, "expert", scatter_dimension=1, tiled=True),
        lax.psum_scatter(padded_out, "expert", scatter_dimension=1, tiled=True),
    )
    summed_in_t, summed_out = (
        lax.psum(group_in_t.astype(jnp.bfloat16), "dp").astype(jnp.float32),
        lax.psum(group_out.astype(jnp.bfloat16), "dp").astype(jnp.float32),
    )
    d_resid_norm, grad_ln2_gain, grad_ln2_shift = ln2_back(d_normed_two)
    d_resid = grad_out + d_resid_norm
    d_branch_b = d_resid.astype(jnp.bfloat16)
    grad_w_attn_out = contract_rows(mixed_b, d_branch_b)
    d_mixed_b = contract_cols(d_branch_b, w_attn_out).astype(jnp.bfloat16)

    def backward_block(state_pair, inputs_block):
        key_grads, value_grads = state_pair
        block_index, lse_block = inputs_block
        block_start = block_index * qblock
        queries, keys_row, values_row, row_start, scores = row_pieces(
            qkv_b, seg_start, block_start, qblock
        )
        attn_probs = jnp.exp(scores - lse_block[:, :, None])
        grad_rows = lax.dynamic_slice_in_dim(d_mixed_b, block_start, qblock, 0).reshape(
            qblock, HEADS, DH
        )
        d_probs = jnp.einsum(
            "qhd,khd->hqk", grad_rows, values_row, preferred_element_type=jnp.float32
        )
        delta_rows = jnp.sum(attn_probs * d_probs, axis=-1, keepdims=True)
        d_scores = (attn_probs * (d_probs - delta_rows)).astype(jnp.bfloat16)
        d_query = (
            jnp.einsum("hqk,khd->qhd", d_scores, keys_row, preferred_element_type=jnp.float32)
            * score_scale
        )
        d_keys = (
            jnp.einsum("hqk,qhd->khd", d_scores, queries, preferred_element_type=jnp.float32)
            * score_scale
        )
        d_values = jnp.einsum(
            "hqk,qhd->khd",
            attn_probs.astype(jnp.bfloat16),
            grad_rows,
            preferred_element_type=jnp.float32,
        )
        old_keys = key_grads
        key_grads = old_keys + d_keys.reshape(LEN, feat_width)
        old_values = value_grads
        value_grads = old_values + d_values.reshape(LEN, feat_width)
        return ((key_grads, value_grads), d_query.reshape(qblock, feat_width))

    empty_grads = jnp.zeros((tok_count, feat_width), jnp.float32)
    (key_grads, value_grads), query_blocks = lax.scan(
        backward_block, (empty_grads, empty_grads), (jnp.arange(n_blocks, dtype=jnp.int32), lse_all)
    )
    query_grads = query_blocks.reshape(tok_count, feat_width)
    d_qkv = (
        jnp.stack([query_grads, key_grads, value_grads], axis=1)
        .reshape(tok_count, 3 * feat_width)
        .astype(jnp.bfloat16)
    )
    grad_w_qkv = contract_rows(normed_one_b, d_qkv)
    d_normed_one = contract_cols(d_qkv, w_qkv)
    d_inputs_norm, grad_ln1_gain, grad_ln1_shift = ln1_back(d_normed_one)
    grad_tokens = d_resid + d_inputs_norm
    modality = dispatch_slot // capacity // group_size
    local_counts = jnp.sum(
        (modality[:, None] == jnp.arange(2, dtype=jnp.int32)[None, :]).astype(jnp.float32), axis=0
    )
    reduced = lax.psum(
        (
            grad_w_qkv,
            grad_w_attn_out,
            grad_ln1_gain,
            grad_ln1_shift,
            grad_ln2_gain,
            grad_ln2_shift,
            local_counts,
        ),
        ("dp", "expert"),
    )
    all_counts = reduced[6]
    factor = jnp.sum(all_counts) / (2.0 * all_counts)
    grad_w_in = jnp.transpose(summed_in_t, (0, 2, 1)) * factor[:, None, None]
    grad_w_out = summed_out * factor[:, None, None]
    return (
        result_out,
        grad_tokens,
        reduced[2],
        reduced[3],
        reduced[0],
        reduced[1],
        reduced[4],
        reduced[5],
        grad_w_in,
        grad_w_out,
        all_counts.astype(jnp.int32),
    )


def solution(mesh):
    return jax.shard_map(
        shards,
        mesh=mesh,
        in_specs=(
            P(("dp", "expert"), None),
            P(("dp", "expert"), None),
            P(("dp", "expert")),
            P(("dp", "expert")),
            P(),
            P(),
            P(),
            P(),
            P(),
            P(),
            P(),
            P(),
        ),
        out_specs=(
            P(("dp", "expert"), None),
            P(("dp", "expert"), None),
            P(),
            P(),
            P(),
            P(),
            P(),
            P(),
            P(None, None, "expert"),
            P(None, "expert", None),
            P(),
        ),
        check_vma=False,
    )
```

profile of v0, /device:TPU:0, one launch (start us, length us, event | category | flops | bytes accessed | tf_op | source)
XLA Modules:
  0.0 1347.1 jit_solution(15896508103572154383)
XLA Ops:
  32.0 92.0 %while.27 = (s32[]{:T(128)}, bf16[2,512,768]{2,1,0:T(8,128)(2,1)}, f32[2,12,512]{2,1,0:T(8,128)}, s32[2]{0:T(128)S(1)}, s32[1024]{0:T(1024)S(1)}, /*index=5*/bf1...) while((s32[]{:T(128)}, bf16[2,512,768]{2,1,0:T(8,128)(2,1)}, ...), condition=%wide.region_5.6_spmd, body=%wide.region_2.5_spmd.sunk | while | flops 1687021568 | bytes 191465728 | solution.py:103
  35.5 12.1 fusion.114
  47.6 12.3 fusion.115
  63.0 9.9 fusion.116
  81.4 12.1 fusion.114
  93.5 12.3 fusion.115
  108.9 9.9 fusion.116
  133.4 11.7 gather_fusion.2
  145.1 11.8 gather_fusion
  168.6 71.1 %all-to-all-done = bf16[8,256,768]{2,1,0:T(8,128)(2,1)} async-done(((bf16[8,256,768]{2,1,0:T(8,128)(2,1)}), bf16[8,256,768]{2,1,0:T(8,128)(2,1)}, u32[]{:S(2)}, u32[]{:S(2)}) %all-to-all-start) | async-done | bytes 3145760 | tf_op jit(solution)/shard_map/all_to_all | solution.py:118
  244.3 64.3 %multiply_convert_fusion.1 = (bf16[2048,3072]{1,0:T(8,128)(2,1)}, f32[2048,3072]{1,0:T(8,128)}, f32[2048,3072]{1,0:T(8,128)}) fusion(bf16[2048,768]{1,0:T(8,128)(2,1)} %bitcast.11, bf16[2,768,3072]{2,1,0:T(8,128)(2,1)} %param.30, s32[]{:T(128)S(6)} %select_n.60), kind=kOutput, calls=%fused_computation.47 | convolution fusion | flops 10072621056 | bytes 70778880 | tf_op jit(solution)/shard_map/dot_general | solution.py:120
  315.8 33.4 %add_convert_fusion = bf16[2048,3072]{1,0:T(8,128)(2,1)} fusion(f32[2048,3072]{1,0:T(8,128)} %get-tuple-element.283, f32[2048,3072]{1,0:T(8,128)} %get-tuple-element.304, bf16[2048,768]{1,0:T(8,128)(2,1)} %bitcast.17, bf16[2,3072,768]{2,1,0:T(8,128)(2,1)} %param.31, s32[]{:T(128)S(6)} %select_n.60), kind=kOutput, calls=%fused_computation.46 | convolution fusion | flops 9751756800 | bytes 70778880 | tf_op jit(solution)/shard_map/dot_general | solution.py:33
  349.2 14.1 %fusion.79 = f32[3072,768]{1,0:T(8,128)S(1)} fusion(bf16[2048,3072]{1,0:T(8,128)(2,1)} %add_convert_fusion, bf16[2048,768]{1,0:T(8,128)(2,1)} %bitcast.11), kind=kOutput, calls=%fused_computation.163 | convolution fusion | flops 9663676416 | bytes 25165824 | tf_op jit(solution)/shard_map/dot_general | solution.py:27
  363.3 14.3 %fusion.80 = f32[3072,768]{1,0:T(8,128)S(1)} fusion(bf16[2048,3072]{1,0:T(8,128)(2,1)} %get-tuple-element.282, bf16[2048,768]{1,0:T(8,128)(2,1)} %bitcast.17), kind=kOutput, calls=%fused_computation.164 | convolution fusion | flops 9663676416 | bytes 25165824 | tf_op jit(solution)/shard_map/dot_general | solution.py:27
  377.6 13.1 broadcast_select_fusion
  391.4 15.5 %fusion.40 = bf16[2048,768]{1,0:T(8,128)(2,1)} fusion(bf16[2048,3072]{1,0:T(8,128)(2,1)} %add_convert_fusion, bf16[2,768,3072]{2,1,0:T(8,128)(2,1)} %param.30, s32[]{:T(128)S(6)} %select_n.60), kind=kOutput, calls=%fused_computation.92 | convolution fusion | flops 9665249280 | bytes 20447236 | tf_op jit(solution)/shard_map/dot_general | solution.py:33
  411.3 15.5 %fusion.43 = bf16[2048,768]{1,0:T(8,128)(2,1)} fusion(bf16[2048,3072]{1,0:T(8,128)(2,1)} %get-tuple-element.282, bf16[2,3072,768]{2,1,0:T(8,128)(2,1)} %param.31, s32[]{:T(128)S(6)} %select_n.60), kind=kOutput, calls=%fused_computation.93 | convolution fusion | flops 9665249280 | bytes 20447236 | tf_op jit(solution)/shard_map/dot_general | solution.py:122
  426.8 110.9 %all-to-all-done.3 = bf16[8,256,768]{2,1,0:T(8,128)(2,1)} async-done(((bf16[8,256,768]{2,1,0:T(8,128)(2,1)}), bf16[8,256,768]{2,1,0:T(8,128)(2,1)}, u32[]{:S(2)}, u32[]{:S(2)}) %all-to-all-start.3) | async-done | bytes 3145760 | tf_op jit(solution)/shard_map/all_to_all | solution.py:148
  546.8 103.8 %all-to-all-done.1 = bf16[8,256,768]{2,1,0:T(8,128)(2,1)} async-done(((bf16[8,256,768]{2,1,0:T(8,128)(2,1)}), bf16[8,256,768]{2,1,0:T(8,128)(2,1)}, u32[]{:S(2)}, u32[]{:S(2)}) %all-to-all-start.1) | async-done | bytes 3145760 | tf_op jit(solution)/shard_map/all_to_all | solution.py:129
  684.3 14.5 %reduce-scatter.5.cloned.1.call-done = f32[2,384,768]{2,1,0:T(8,128)} async-done(((f32[2,3072,768]{2,1,0:T(8,128)}), f32[2,384,768]{2,1,0:T(8,128)}) %reduce-scatter.5.cloned.1.call-update) | async-done | bytes 2359312 | tf_op jit(solution)/shard_map/reduce_scatter | solution.py:167
  701.6 198.7 %reduce-scatter.3.cloned.1.call-done = f32[2,384,768]{2,1,0:T(8,128)} async-done(((f32[2,3072,768]{2,1,0:T(8,128)}), f32[2,384,768]{2,1,0:T(8,128)}) %reduce-scatter.3.cloned.1.call-update) | async-done | bytes 2359312 | tf_op jit(solution)/shard_map/reduce_scatter | solution.py:166
  903.3 209.2 %while.28 = (s32[]{:T(128)}, f32[1024,768]{0,1:T(8,128)}, f32[1024,768]{0,1:T(8,128)}, bf16[2,512,768]{2,1,0:T(8,128)(2,1)}, s32[2]{0:T(128)S(1)}, /*index=5*/bf...) while((s32[]{:T(128)}, f32[1024,768]{0,1:T(8,128)}, ...), condition=%wide.region_13.16_spmd.clone, body=%wide.region_11.15_spmd.clone.sunk | while | flops 4126140416 | bytes 332425696 | solution.py:216
  915.7 10.3 fusion.122
  926.0 13.5 %fusion.123 = f32[12,64,1024]{2,1,0:T(8,128)} fusion(bf16[512,12,64]{0,2,1:T(8,128)(2,1)S(1)} %bitcast.171, f32[12,512,1024]{2,1,0:T(8,128)} %fusion.122, f32[12,512]{1,0:T(8,128)S(1)} %copy-done.21, pred[512,1024]{1,0:T(8,128)(4,1)S(1)} %copy-done.4), kind=kOutput, calls=%fused_computation.26.clone.1 | convolution fusion | flops 830472192 | bytes 29646848 | tf_op jit(solution)/shard_map/while/body/eval_jaxpr/hqk,qhd->khd/dot_general | solution.py:203
  939.5 18.9 %multiply_reduce_fusion.3 = (f32[12,512]{1,0:T(8,128)}, f32[12,512,1024]{2,1,0:T(8,128)}) fusion(f32[12,512,1024]{2,1,0:T(8,128)} %fusion.122, f32[12,512]{1,0:T(8,128)} %dynamic-slice_bitcast_fusion.2, pred[512,1024]{1,0:T(8,128)(4,1)} %broadcast_compare_fusion.5, bf16[512,12,64]{0,2,1:T(8,128)(2,1)} %bitcast.170, ...), kind=kOutput, calls=%fused_computation.23.clone.1 | convolution fusion | flops 836757504 | bytes 53272576 | tf_op jit(solution)/shard_map/while/body/eval_jaxpr/qhd,khd->hqk/dot_general | solution.py:190
  958.4 23.4 %multiply_convert_fusion.3 = bf16[12,512,1024]{2,1,0:T(8,128)(2,1)} fusion(f32[12,512,1024]{2,1,0:T(8,128)} %get-tuple-element.406, f32[12,512,1024]{2,1,0:T(8,128)} %fusion.122, f32[12,512]{1,0:T(8,128)} %get-tuple-element.407, f32[12,512]{1,0:T(8,128)} %dynamic-slice_bitcast_fusion.2, pred[512,1024]{1,0:T(8,128)(4,1)} %broadcast_compare_fusion.5), kind=kLoop, calls=%fused_computation.22.clone.1 | loop fusion | flops 37748736 | bytes 63488000 | tf_op jit(solution)/shard_map/while/body/eval_jaxpr/convert_element_type | solution.py:194
  1020.8 10.1 fusion.122
  1030.9 13.1 fusion.123
  1044.0 18.8 %multiply_reduce_fusion.3 = (f32[12,512]{1,0:T(8,128)}, f32[12,512,1024]{2,1,0:T(8,128)}) fusion(f32[12,512,1024]{2,1,0:T(8,128)} %fusion.122, f32[12,512]{1,0:T(8,128)} %dynamic-slice_bitcast_fusion.2, pred[512,1024]{1,0:T(8,128)(4,1)} %broadcast_compare_fusion.5, bf16[512,12,64]{0,2,1:T(8,128)(2,1)} %bitcast.170, ...), kind=kOutput, calls=%fused_computation.23.clone.1 | convolution fusion | flops 836757504 | bytes 53272576 | tf_op jit(solution)/shard_map/while/body/eval_jaxpr/qhd,khd->hqk/dot_general | solution.py:190
  1062.8 22.2 %multiply_convert_fusion.3 = bf16[12,512,1024]{2,1,0:T(8,128)(2,1)} fusion(f32[12,512,1024]{2,1,0:T(8,128)} %get-tuple-element.406, f32[12,512,1024]{2,1,0:T(8,128)} %fusion.122, f32[12,512]{1,0:T(8,128)} %get-tuple-element.407, f32[12,512]{1,0:T(8,128)} %dynamic-slice_bitcast_fusion.2, pred[512,1024]{1,0:T(8,128)(4,1)} %broadcast_compare_fusion.5), kind=kLoop, calls=%fused_computation.22.clone.1 | loop fusion | flops 37748736 | bytes 63488000 | tf_op jit(solution)/shard_map/while/body/eval_jaxpr/convert_element_type | solution.py:194
  1154.3 39.8 %all-reduce.4 = (f32[768]{0:T(1024)}, f32[768]{0:T(1024)}, f32[768]{0:T(1024)}, f32[768]{0:T(1024)}, f32[2]{0:T(128)}) all-reduce(f32[768]{0:T(1024)} %get-tuple-element.234, f32[768]{0:T(1024)} %get-tuple-element.238, f32[768]{0:T(1024)} %get-tuple-element.236, ...), channel_id=1, replica_groups=mesh['dp'=4,'expert'=8] {'dp','expert'}, use_global_device_ids=true, to_apply=%region_17.20 | all-reduce | flops 3074 | bytes 24592 | tf_op jit(solution)/shard_map/psum | solution.py:233
  1211.5 120.9 %all-reduce.10.cloned.1.call-done = (f32[768,2304]{1,0:T(8,128)}, f32[768,768]{1,0:T(8,128)}) async-done(((f32[768,2304]{1,0:T(8,128)}, f32[768,768]{1,0:T(8,128)}), (f32[768,2304]{1,0:T(8,128)}, f32[768,768]{1,0:T(8,128)})) %all-reduce.10.cloned.1.call-update) | async-done | bytes 9437200 | tf_op jit(solution)/shard_map/psum | solution.py:233
  (254 shorter events, 276.9 us)
Async XLA Ops:
  7.2 12.2 copy-start
  7.2 12.2 copy-start.47
  47.6 15.4 %copy-start.1 = (f32[12,512,1024]{2,1,0:T(8,128)S(1)}, f32[12,512,1024]{2,1,0:T(8,128)}, u32[]{:S(2)}) copy-start(f32[12,512,1024]{2,1,0:T(8,128)} %get-tuple-element.395) | copy-start | bytes 75497472 | tf_op jit(solution)/shard_map/while
  63.0 9.9 copy-start.27
  93.5 15.4 %copy-start.1 = (f32[12,512,1024]{2,1,0:T(8,128)S(1)}, f32[12,512,1024]{2,1,0:T(8,128)}, u32[]{:S(2)}) copy-start(f32[12,512,1024]{2,1,0:T(8,128)} %get-tuple-element.395) | copy-start | bytes 75497472 | tf_op jit(solution)/shard_map/while
  108.9 9.9 copy-start.27
  145.1 11.8 copy-start.53
  161.8 78.0 %all-to-all-start = ((bf16[8,256,768]{2,1,0:T(8,128)(2,1)}), bf16[8,256,768]{2,1,0:T(8,128)(2,1)}, u32[]{:S(2)}, u32[]{:S(2)}) async-start(bf16[8,256,768]{2,1,0:T(8,128)(2,1)} %bitcast.175), calls=%async_computation | async-start | bytes 6291456 | tf_op jit(solution)/shard_map/all_to_all | solution.py:118
  239.8 76.0 %all-to-all-start.2 = ((bf16[8,256,768]{2,1,0:T(8,128)(2,1)}), bf16[8,256,768]{2,1,0:T(8,128)(2,1)}, u32[]{:S(2)}, u32[]{:S(2)}) async-start(bf16[8,256,768]{2,1,0:T(8,128)(2,1)} %bitcast.174), calls=%async_computation.2 | async-start | bytes 6291456 | tf_op jit(solution)/shard_map/all_to_all | solution.py:140
  244.2 454.6 %reduce-scatter.5.cloned.1.call-start = ((), (), s32[]{:S(2)}) async-start(), calls=%async_computation.7 | async-start | bytes 21233664 | tf_op jit(solution)/shard_map/reduce_scatter | solution.py:167
  363.3 14.3 %copy-start.55 = (pred[2]{0:T(512)(128)(4,1)S(1)}, pred[2]{0:T(512)(128)(4,1)}, u32[]{:S(2)}) copy-start(pred[2]{0:T(512)(128)(4,1)} %iota_compare_fusion) | copy-start | bytes 10
  390.7 509.7 %reduce-scatter.3.cloned.1.call-start = ((), (), s32[]{:S(2)}) async-start(), calls=%async_computation.6 | async-start | bytes 21233664 | tf_op jit(solution)/shard_map/reduce_scatter | solution.py:166
  406.9 130.8 %all-to-all-start.3 = ((bf16[8,256,768]{2,1,0:T(8,128)(2,1)}), bf16[8,256,768]{2,1,0:T(8,128)(2,1)}, u32[]{:S(2)}, u32[]{:S(2)}) async-start(bf16[8,256,768]{2,1,0:T(8,128)(2,1)} %bitcast.181), calls=%async_computation.3 | async-start | bytes 6291456 | tf_op jit(solution)/shard_map/all_to_all | solution.py:148
  537.7 112.8 %all-to-all-start.1 = ((bf16[8,256,768]{2,1,0:T(8,128)(2,1)}), bf16[8,256,768]{2,1,0:T(8,128)(2,1)}, u32[]{:S(2)}, u32[]{:S(2)}) async-start(bf16[8,256,768]{2,1,0:T(8,128)(2,1)} %bitcast.180), calls=%async_computation.1 | async-start | bytes 6291456 | tf_op jit(solution)/shard_map/all_to_all | solution.py:129
  542.4 661.7 %all-reduce.12.cloned.1.call-start = ((), (), s32[]{:S(2)}) async-start(), calls=%async_computation.9 | async-start | bytes 4718592 | tf_op jit(solution)/shard_map/psum | solution.py:170
  662.2 7.9 copy-start.30
  662.2 7.9 copy-start.35
  662.2 7.9 copy-start.43
  701.6 201.7 %copy-start.26 = (s32[1024]{0:T(1024)S(1)}, s32[1024]{0:T(1024)}, u32[]{:S(2)}) copy-start(s32[1024]{0:T(1024)} %param.22) | copy-start | bytes 12292
  903.2 429.2 %all-reduce.10.cloned.1.call-start = ((), (), s32[]{:S(2)}) async-start(), calls=%async_computation.8 | async-start | bytes 18874368 | tf_op jit(solution)/shard_map/psum | solution.py:233
  915.7 10.3 copy-start.4
  915.7 10.3 copy-start.10
  915.7 10.3 copy-start.21
  991.6 7.6 copy-start.9
  1020.8 10.1 copy-start.4
  1020.8 10.1 copy-start.10
  1020.8 10.1 copy-start.21
  1094.8 7.6 copy-start.9
  1143.2 8.7 copy-start.39
  1143.2 8.7 copy-start.16
  1143.2 8.7 copy-start.49
  1151.9 46.0 %copy-start.45 = (f32[1024]{0:T(1024)S(1)}, f32[1024]{0:T(1024)}, u32[]{:S(2)}) copy-start(f32[1024]{0:T(1024)} %copy-done.44) | copy-start | bytes 12292
  (48 other events, 166.6 us)
Sparse Core Ops, SparseCore 0:
  390.8 307.9 reduce-scatter.4
  701.2 199.1 reduce-scatter.2
  903.5 72.5 all-reduce.11
  1142.0 190.3 all-reduce.9
where the time goes:
time: 1360 us; the launch traced here: 1350 us
  waiting for transfers between devices  628 us (46%)
  matrix products  352 us (26%)
  local copies, waits for them, and re-layouts  147 us (11%)
  other arithmetic  142 us (10%)
  blocking collectives  39.8 us (3%)
  starting transfers between devices  20 us (1%)
  between operations  14.5 us (1%)
    reduce_scatter x1, waiting for transfers between devices, shards(): lax.psum_scatter(padded_in, 'expert', scatter_dimension=1, tiled=True)  199 us
    psum x1, waiting for transfers between devices, shards(): lax.psum((grad_w_qkv, grad_w_attn_out, grad_ln1_gain, grad_ln1_shift, gra...  121 us
    all_to_all x1, waiting for transfers between devices, shards(): lax.all_to_all(d_rows.reshape(n_expert, capacity, feat_width), 'expert',...  111 us
    all_to_all x1, waiting for transfers between devices, shards(): lax.all_to_all(expert_rows_b, 'expert', split_axis=0, concat_axis=0, tile...  104 us
    all_to_all x1, waiting for transfers between devices, shards(): lax.all_to_all(send_rows, 'expert', split_axis=0, concat_axis=0, tiled=True)  71.1 us
    dot_general x1, matrix products, shards(): jnp.dot(flat_rows, expert_in, preferred_element_type=jnp.float32)  64.3 us
    dot_general x4, matrix products, contract_cols(): lax.dot_general(first_op, second_op, (((1,), (1,)), ((), ())), preferred_...  60.2 us
    convert_element_type x2, other arithmetic, backward_block(): d_scores = (attn_probs * (d_probs - delta_rows)).astype(jnp.bfloat16)  45.5 us
  transfers between devices with their start and end apart: 8, of which 7 were waited for; matrix products, arithmetic and copies ran while one was open for 29% of the time, Pallas kernels for 0%

commit v1 on v0

--- a/solution.py
+++ b/solution.py
@@ -231,16 +231,19 @@
         (modality[:, None] == jnp.arange(2, dtype=jnp.int32)[None, :]).astype(jnp.float32), axis=0
     )
     reduced = lax.psum(
-        (
-            grad_w_qkv,
-            grad_w_attn_out,
-            grad_ln1_gain,
-            grad_ln1_shift,
-            grad_ln2_gain,
-            grad_ln2_shift,
-            local_counts,
+        lax.psum(
+            (
+                grad_w_qkv,
+                grad_w_attn_out,
+                grad_ln1_gain,
+                grad_ln1_shift,
+                grad_ln2_gain,
+                grad_ln2_shift,
+                local_counts,
+            ),
+            axis_name="expert",
         ),
-        ("dp", "expert"),
+        axis_name="dp",
     )
     all_counts = reduced[6]
     factor = jnp.sum(all_counts) / (2.0 * all_counts)

time: 1360 us -> 1420 us (1.044)
  waiting for transfers between devices: 628 us -> 682 us
    reduce_scatter x1, waiting for transfers between devices: 199 us -> 0.01 us  [shards(): lax.psum_scatter(padded_in, 'expert', scatter_dimension=1, tiled=True)]
    psum x0 -> x1, waiting for transfers between devices: none -> 186 us  [shards(): lax.psum(lax.psum((grad_w_qkv, grad_w_attn_out, grad_ln1_gain, grad_ln1_s...]
    psum x1, waiting for transfers between devices: 121 us -> 192 us  [shards(): lax.psum((grad_w_qkv, grad_w_attn_out, grad_ln1_gain, grad_ln1_shift, gra...]
    psum x0 -> x1, blocking collectives: none -> 17.9 us  [shards(): lax.psum(lax.psum((grad_w_qkv, grad_w_attn_out, grad_ln1_gain, grad_ln1_s...]
    reduce_scatter x1, waiting for transfers between devices: 14.5 us -> 0.02 us  [shards(): lax.psum_scatter(padded_out, 'expert', scatter_dimension=1, tiled=True)]
  transfers between devices with their start and end apart: 8 -> 9, of which waited for: 7 -> 7; matrix products, arithmetic and copies ran while one was open for 29% -> 28% of each run, Pallas kernels for 0% -> 0%
where the time goes in v1:
time: 1420 us; the launch traced here: 1410 us
  waiting for transfers between devices  682 us (48%)
  matrix products  352 us (25%)
  local copies, waits for them, and re-layouts  147 us (10%)
  other arithmetic  141 us (10%)
  blocking collectives  47 us (3%)
  starting transfers between devices  20.1 us (1%)
  between operations  14.5 us (1%)
    psum x1, waiting for transfers between devices, shards(): lax.psum((grad_w_qkv, grad_w_attn_out, grad_ln1_gain, grad_ln1_shift, gra...  192 us
    psum x1, waiting for transfers between devices, shards(): lax.psum(lax.psum((grad_w_qkv, grad_w_attn_out, grad_ln1_gain, grad_ln1_s...  186 us
    all_to_all x1, waiting for transfers between devices, shards(): lax.all_to_all(d_rows.reshape(n_expert, capacity, feat_width), 'expert',...  111 us
    all_to_all x1, waiting for transfers between devices, shards(): lax.all_to_all(expert_rows_b, 'expert', split_axis=0, concat_axis=0, tile...  105 us
    all_to_all x1, waiting for transfers between devices, shards(): lax.all_to_all(send_rows, 'expert', split_axis=0, concat_axis=0, tiled=True)  71.1 us
    dot_general x1, matrix products, shards(): jnp.dot(flat_rows, expert_in, preferred_element_type=jnp.float32)  64.3 us
    dot_general x4, matrix products, contract_cols(): lax.dot_general(first_op, second_op, (((1,), (1,)), ((), ())), preferred_...  59.2 us
    convert_element_type x2, other arithmetic, backward_block(): d_scores = (attn_probs * (d_probs - delta_rows)).astype(jnp.bfloat16)  45 us
  transfers between devices with their start and end apart: 9, of which 7 were waited for; matrix products, arithmetic and copies ran while one was open for 28% of the time, Pallas kernels for 0%

profile of v1, /device:TPU:0, one launch (start us, length us, event | category | flops | bytes accessed | tf_op | source)
XLA Modules:
  0.0 1407.5 jit_solution(5303062303153715847)
XLA Ops:
  31.9 91.7 %while.27 = (s32[]{:T(128)}, bf16[2,512,768]{2,1,0:T(8,128)(2,1)}, f32[2,12,512]{2,1,0:T(8,128)}, s32[2]{0:T(128)S(1)}, s32[1024]{0:T(1024)S(1)}, /*index=5*/bf1...) while((s32[]{:T(128)}, bf16[2,512,768]{2,1,0:T(8,128)(2,1)}, ...), condition=%wide.region_5.6_spmd, body=%wide.region_2.5_spmd.sunk | while | flops 1687021568 | bytes 191465728 | solution.py:103
  35.4 12.0 fusion.114
  47.4 12.3 fusion.115
  62.8 9.9 fusion.116
  81.2 12.0 fusion.114
  93.2 12.3 fusion.115
  108.6 9.9 fusion.116
  133.1 11.7 gather_fusion.2
  144.8 11.7 gather_fusion
  168.3 71.1 %all-to-all-done = bf16[8,256,768]{2,1,0:T(8,128)(2,1)} async-done(((bf16[8,256,768]{2,1,0:T(8,128)(2,1)}), bf16[8,256,768]{2,1,0:T(8,128)(2,1)}, u32[]{:S(2)}, u32[]{:S(2)}) %all-to-all-start) | async-done | bytes 3145760 | tf_op jit(solution)/shard_map/all_to_all | solution.py:118
  244.0 64.3 %multiply_convert_fusion.1 = (bf16[2048,3072]{1,0:T(8,128)(2,1)}, f32[2048,3072]{1,0:T(8,128)}, f32[2048,3072]{1,0:T(8,128)}) fusion(bf16[2048,768]{1,0:T(8,128)(2,1)} %bitcast.11, bf16[2,768,3072]{2,1,0:T(8,128)(2,1)} %param.30, s32[]{:T(128)S(6)} %select_n.60), kind=kOutput, calls=%fused_computation.47 | convolution fusion | flops 10072621056 | bytes 70778880 | tf_op jit(solution)/shard_map/dot_general | solution.py:120
  315.4 33.1 %add_convert_fusion = bf16[2048,3072]{1,0:T(8,128)(2,1)} fusion(f32[2048,3072]{1,0:T(8,128)} %get-tuple-element.290, f32[2048,3072]{1,0:T(8,128)} %get-tuple-element.311, bf16[2048,768]{1,0:T(8,128)(2,1)} %bitcast.17, bf16[2,3072,768]{2,1,0:T(8,128)(2,1)} %param.31, s32[]{:T(128)S(6)} %select_n.60), kind=kOutput, calls=%fused_computation.46 | convolution fusion | flops 9751756800 | bytes 70778880 | tf_op jit(solution)/shard_map/dot_general | solution.py:33
  348.5 14.1 %fusion.79 = f32[3072,768]{1,0:T(8,128)S(1)} fusion(bf16[2048,3072]{1,0:T(8,128)(2,1)} %add_convert_fusion, bf16[2048,768]{1,0:T(8,128)(2,1)} %bitcast.11), kind=kOutput, calls=%fused_computation.163 | convolution fusion | flops 9663676416 | bytes 25165824 | tf_op jit(solution)/shard_map/dot_general | solution.py:27
  362.6 14.3 %fusion.80 = f32[3072,768]{1,0:T(8,128)S(1)} fusion(bf16[2048,3072]{1,0:T(8,128)(2,1)} %get-tuple-element.289, bf16[2048,768]{1,0:T(8,128)(2,1)} %bitcast.17), kind=kOutput, calls=%fused_computation.164 | convolution fusion | flops 9663676416 | bytes 25165824 | tf_op jit(solution)/shard_map/dot_general | solution.py:27
  377.0 12.8 broadcast_select_fusion
  390.5 15.5 %fusion.40 = bf16[2048,768]{1,0:T(8,128)(2,1)} fusion(bf16[2048,3072]{1,0:T(8,128)(2,1)} %add_convert_fusion, bf16[2,768,3072]{2,1,0:T(8,128)(2,1)} %param.30, s32[]{:T(128)S(6)} %select_n.60), kind=kOutput, calls=%fused_computation.92 | convolution fusion | flops 9665249280 | bytes 20447236 | tf_op jit(solution)/shard_map/dot_general | solution.py:33
  410.5 15.5 %fusion.43 = bf16[2048,768]{1,0:T(8,128)(2,1)} fusion(bf16[2048,3072]{1,0:T(8,128)(2,1)} %get-tuple-element.289, bf16[2,3072,768]{2,1,0:T(8,128)(2,1)} %param.31, s32[]{:T(128)S(6)} %select_n.60), kind=kOutput, calls=%fused_computation.93 | convolution fusion | flops 9665249280 | bytes 20447236 | tf_op jit(solution)/shard_map/dot_general | solution.py:122
  426.0 110.8 %all-to-all-done.3 = bf16[8,256,768]{2,1,0:T(8,128)(2,1)} async-done(((bf16[8,256,768]{2,1,0:T(8,128)(2,1)}), bf16[8,256,768]{2,1,0:T(8,128)(2,1)}, u32[]{:S(2)}, u32[]{:S(2)}) %all-to-all-start.3) | async-done | bytes 3145760 | tf_op jit(solution)/shard_map/all_to_all | solution.py:148
  545.9 104.9 %all-to-all-done.1 = bf16[8,256,768]{2,1,0:T(8,128)(2,1)} async-done(((bf16[8,256,768]{2,1,0:T(8,128)(2,1)}), bf16[8,256,768]{2,1,0:T(8,128)(2,1)}, u32[]{:S(2)}, u32[]{:S(2)}) %all-to-all-start.1) | async-done | bytes 3145760 | tf_op jit(solution)/shard_map/all_to_all | solution.py:129
  683.8 209.6 %while.28 = (s32[]{:T(128)}, f32[1024,768]{0,1:T(8,128)}, f32[1024,768]{0,1:T(8,128)}, bf16[2,512,768]{2,1,0:T(8,128)(2,1)}, s32[2]{0:T(128)S(1)}, /*index=5*/bf...) while((s32[]{:T(128)}, f32[1024,768]{0,1:T(8,128)}, ...), condition=%wide.region_13.16_spmd.clone, body=%wide.region_11.15_spmd.clone.sunk | while | flops 4126140416 | bytes 332425696 | solution.py:216
  696.2 10.2 fusion.122
  706.5 13.1 fusion.123
  719.5 18.8 %multiply_reduce_fusion.3 = (f32[12,512]{1,0:T(8,128)}, f32[12,512,1024]{2,1,0:T(8,128)}) fusion(f32[12,512,1024]{2,1,0:T(8,128)} %fusion.122, f32[12,512]{1,0:T(8,128)} %dynamic-slice_bitcast_fusion.2, pred[512,1024]{1,0:T(8,128)(4,1)} %broadcast_compare_fusion.5, bf16[512,12,64]{0,2,1:T(8,128)(2,1)} %bitcast.170, ...), kind=kOutput, calls=%fused_computation.23.clone.1 | convolution fusion | flops 836757504 | bytes 53272576 | tf_op jit(solution)/shard_map/while/body/eval_jaxpr/qhd,khd->hqk/dot_general | solution.py:190
  738.3 22.5 %multiply_convert_fusion.3 = bf16[12,512,1024]{2,1,0:T(8,128)(2,1)} fusion(f32[12,512,1024]{2,1,0:T(8,128)} %get-tuple-element.413, f32[12,512,1024]{2,1,0:T(8,128)} %fusion.122, f32[12,512]{1,0:T(8,128)} %get-tuple-element.414, f32[12,512]{1,0:T(8,128)} %dynamic-slice_bitcast_fusion.2, pred[512,1024]{1,0:T(8,128)(4,1)} %broadcast_compare_fusion.5), kind=kLoop, calls=%fused_computation.22.clone.1 | loop fusion | flops 37748736 | bytes 63488000 | tf_op jit(solution)/shard_map/while/body/eval_jaxpr/convert_element_type | solution.py:194
  800.2 10.8 fusion.122
  810.9 13.3 fusion.123
  824.3 18.9 %multiply_reduce_fusion.3 = (f32[12,512]{1,0:T(8,128)}, f32[12,512,1024]{2,1,0:T(8,128)}) fusion(f32[12,512,1024]{2,1,0:T(8,128)} %fusion.122, f32[12,512]{1,0:T(8,128)} %dynamic-slice_bitcast_fusion.2, pred[512,1024]{1,0:T(8,128)(4,1)} %broadcast_compare_fusion.5, bf16[512,12,64]{0,2,1:T(8,128)(2,1)} %bitcast.170, ...), kind=kOutput, calls=%fused_computation.23.clone.1 | convolution fusion | flops 836757504 | bytes 53272576 | tf_op jit(solution)/shard_map/while/body/eval_jaxpr/qhd,khd->hqk/dot_general | solution.py:190
  843.2 22.5 %multiply_convert_fusion.3 = bf16[12,512,1024]{2,1,0:T(8,128)(2,1)} fusion(f32[12,512,1024]{2,1,0:T(8,128)} %get-tuple-element.413, f32[12,512,1024]{2,1,0:T(8,128)} %fusion.122, f32[12,512]{1,0:T(8,128)} %get-tuple-element.414, f32[12,512]{1,0:T(8,128)} %dynamic-slice_bitcast_fusion.2, pred[512,1024]{1,0:T(8,128)(4,1)} %broadcast_compare_fusion.5), kind=kLoop, calls=%fused_computation.22.clone.1 | loop fusion | flops 37748736 | bytes 63488000 | tf_op jit(solution)/shard_map/while/body/eval_jaxpr/convert_element_type | solution.py:194
  928.7 192.2 %all-reduce.13.cloned.1.call-done = (f32[768,2304]{1,0:T(8,128)}, f32[768,768]{1,0:T(8,128)}) async-done(((f32[768,2304]{1,0:T(8,128)}, f32[768,768]{1,0:T(8,128)}), (f32[768,2304]{1,0:T(8,128)}, f32[768,768]{1,0:T(8,128)})) %all-reduce.13.cloned.1.call-update) | async-done | bytes 9437200 | tf_op jit(solution)/shard_map/psum | solution.py:234
  1132.7 29.1 %all-reduce.4 = (f32[768]{0:T(1024)}, f32[768]{0:T(1024)}, f32[768]{0:T(1024)}, f32[768]{0:T(1024)}, f32[2]{0:T(128)}) all-reduce(f32[768]{0:T(1024)} %get-tuple-element.234, f32[768]{0:T(1024)} %get-tuple-element.238, f32[768]{0:T(1024)} %get-tuple-element.236, ...), channel_id=1, replica_groups=mesh['dp'=4,'expert'=8] {'expert'}, use_global_device_ids=true, to_apply=%region_17.20 | all-reduce | flops 3074 | bytes 24592 | tf_op jit(solution)/shard_map/psum | solution.py:234
  1161.8 17.9 %all-reduce.6 = (f32[768]{0:T(1024)}, f32[768]{0:T(1024)}, f32[768]{0:T(1024)}, f32[768]{0:T(1024)}, f32[2]{0:T(128)}) all-reduce(f32[768]{0:T(1024)} %get-tuple-element.271, f32[768]{0:T(1024)} %get-tuple-element.272, f32[768]{0:T(1024)} %get-tuple-element.273, ...), channel_id=1, replica_groups=mesh['dp'=4,'expert'=8] {'dp'}, use_global_device_ids=true, to_apply=%region_18.21 | all-reduce | flops 3074 | bytes 24592 | tf_op jit(solution)/shard_map/psum | solution.py:233
  1206.8 185.9 %all-reduce.15.cloned.1.call-done = (f32[768,2304]{1,0:T(8,128)}, f32[768,768]{1,0:T(8,128)}) async-done(((f32[768,2304]{1,0:T(8,128)}, f32[768,768]{1,0:T(8,128)}), (f32[768,2304]{1,0:T(8,128)}, f32[768,768]{1,0:T(8,128)})) %all-reduce.15.cloned.1.call-update) | async-done | bytes 9437200 | tf_op jit(solution)/shard_map/psum | solution.py:233
  (258 shorter events, 286.1 us)
Async XLA Ops:
  7.2 12.2 copy-start
  7.2 12.2 copy-start.47
  47.4 15.4 %copy-start.1 = (f32[12,512,1024]{2,1,0:T(8,128)S(1)}, f32[12,512,1024]{2,1,0:T(8,128)}, u32[]{:S(2)}) copy-start(f32[12,512,1024]{2,1,0:T(8,128)} %get-tuple-element.402) | copy-start | bytes 75497472 | tf_op jit(solution)/shard_map/while
  62.8 9.9 copy-start.27
  93.2 15.4 %copy-start.1 = (f32[12,512,1024]{2,1,0:T(8,128)S(1)}, f32[12,512,1024]{2,1,0:T(8,128)}, u32[]{:S(2)}) copy-start(f32[12,512,1024]{2,1,0:T(8,128)} %get-tuple-element.402) | copy-start | bytes 75497472 | tf_op jit(solution)/shard_map/while
  108.6 9.9 copy-start.27
  144.8 11.7 copy-start.53
  161.5 78.0 %all-to-all-start = ((bf16[8,256,768]{2,1,0:T(8,128)(2,1)}), bf16[8,256,768]{2,1,0:T(8,128)(2,1)}, u32[]{:S(2)}, u32[]{:S(2)}) async-start(bf16[8,256,768]{2,1,0:T(8,128)(2,1)} %bitcast.175), calls=%async_computation | async-start | bytes 6291456 | tf_op jit(solution)/shard_map/all_to_all | solution.py:118
  239.4 76.0 %all-to-all-start.2 = ((bf16[8,256,768]{2,1,0:T(8,128)(2,1)}), bf16[8,256,768]{2,1,0:T(8,128)(2,1)}, u32[]{:S(2)}, u32[]{:S(2)}) async-start(bf16[8,256,768]{2,1,0:T(8,128)(2,1)} %bitcast.174), calls=%async_computation.2 | async-start | bytes 6291456 | tf_op jit(solution)/shard_map/all_to_all | solution.py:140
  243.9 679.1 %reduce-scatter.5.cloned.1.call-start = ((), (), s32[]{:S(2)}) async-start(), calls=%async_computation.7 | async-start | bytes 21233664 | tf_op jit(solution)/shard_map/reduce_scatter | solution.py:167
  362.6 14.3 %copy-start.55 = (pred[2]{0:T(512)(128)(4,1)S(1)}, pred[2]{0:T(512)(128)(4,1)}, u32[]{:S(2)}) copy-start(pred[2]{0:T(512)(128)(4,1)} %iota_compare_fusion) | copy-start | bytes 10
  389.8 536.0 %reduce-scatter.3.cloned.1.call-start = ((), (), s32[]{:S(2)}) async-start(), calls=%async_computation.6 | async-start | bytes 21233664 | tf_op jit(solution)/shard_map/reduce_scatter | solution.py:166
  406.0 130.8 %all-to-all-start.3 = ((bf16[8,256,768]{2,1,0:T(8,128)(2,1)}), bf16[8,256,768]{2,1,0:T(8,128)(2,1)}, u32[]{:S(2)}, u32[]{:S(2)}) async-start(bf16[8,256,768]{2,1,0:T(8,128)(2,1)} %bitcast.181), calls=%async_computation.3 | async-start | bytes 6291456 | tf_op jit(solution)/shard_map/all_to_all | solution.py:148
  536.8 113.9 %all-to-all-start.1 = ((bf16[8,256,768]{2,1,0:T(8,128)(2,1)}), bf16[8,256,768]{2,1,0:T(8,128)(2,1)}, u32[]{:S(2)}, u32[]{:S(2)}) async-start(bf16[8,256,768]{2,1,0:T(8,128)(2,1)} %bitcast.180), calls=%async_computation.1 | async-start | bytes 6291456 | tf_op jit(solution)/shard_map/all_to_all | solution.py:129
  541.5 579.5 %all-reduce.13.cloned.1.call-start = ((), (), s32[]{:S(2)}) async-start(), calls=%async_computation.8 | async-start | bytes 18874368 | tf_op jit(solution)/shard_map/psum | solution.py:234
  662.5 7.9 copy-start.30
  662.5 7.9 copy-start.35
  662.5 7.9 copy-start.43
  696.2 10.2 copy-start.4
  696.2 10.2 copy-start.10
  696.2 10.2 copy-start.21
  770.7 7.8 copy-start.9
  800.1 10.8 copy-start.4
  800.1 10.8 copy-start.10
  800.1 10.8 copy-start.21
  875.5 7.8 copy-start.9
  922.9 276.6 %all-reduce.17.cloned.1.call-start = ((), (), s32[]{:S(2)}) async-start(), calls=%async_computation.10 | async-start | bytes 4718592 | tf_op jit(solution)/shard_map/psum | solution.py:170
  928.6 464.1 %all-reduce.15.cloned.1.call-start = ((), (), s32[]{:S(2)}) async-start(), calls=%async_computation.9 | async-start | bytes 18874368 | tf_op jit(solution)/shard_map/psum | solution.py:233
  1122.2 8.1 copy-start.39
  1122.2 8.1 copy-start.16
  1122.2 8.1 copy-start.49
  1130.3 53.2 %copy-start.45 = (f32[1024]{0:T(1024)S(1)}, f32[1024]{0:T(1024)}, u32[]{:S(2)}) copy-start(f32[1024]{0:T(1024)} %copy-done.44) | copy-start | bytes 12292
  (49 other events, 170.0 us)
Sparse Core Ops, SparseCore 0:
  389.9 308.6 reduce-scatter.4
  700.9 198.4 reduce-scatter.2
  923.1 197.8 all-reduce.12
  1125.0 74.4 all-reduce.16
  1203.5 189.1 all-reduce.14
